TPU v7x, 256 devices: a whole 4x4x8 slice. The times are simulated.
256 devices in a mesh: ka: 8 (over y_lo, x), pw: 32 (over y_hi, z, core).
Axes of the slice: x: 4, y: 4 (y_hi: 2, y_lo: 2; y = y_hi * 2 + y_lo), z: 8, core: 2. Of those that a mesh axis runs over, the one named last changes fastest.
Arguments:
- states_re: bfloat16 [16, 512, 32768], P('ka', None, 'pw'), may hold values from -0.016572815 to 0.016572815
- states_im: bfloat16 [16, 512, 32768], P('ka', None, 'pw'), may hold values from -0.016572815 to 0.016572815
Outputs:
- wilson_lines: float32 [16, 512, 2, 512], P('ka', 'pw')
All inputs are finite; a program needn't handle non-finite values.
Results may differ from a plain program's by a relative error of at most 0.0003.
Values may be sent and summed in bfloat16 or wider, within the bound.
A program may use at most 64 MiB of HBM per device.

v0:
```python
import jax
import jax.numpy as jnp
from jax import lax
from jax.sharding import PartitionSpec as P


def from_behind(block, axis, distance):
    devices = range(lax.axis_size(axis))
    route = [((i - distance) % len(devices), i) for i in devices]
    return lax.ppermute(block, axis, route)


def shifted(shard, axis, by):
    size = lax.axis_size(axis)
    pairs = [(i, i + by) for i in range(size) if 0 <= i + by < size]
    return lax.ppermute(shard, axis, pairs)


def complex_rows(left, right):
    highest = lax.Precision.HIGHEST
    left_re = left[:, 0]
    left_im = left[:, 1]
    right_re = right[:, 0]
    right_im = right[:, 1]
    real_part = jnp.dot(
        left_re, right_re, precision=highest, preferred_element_type=jnp.float32
    ) - jnp.dot(left_im, right_im, precision=highest, preferred_element_type=jnp.float32)
    imag_part = jnp.dot(
        left_re, right_im, precision=highest, preferred_element_type=jnp.float32
    ) + jnp.dot(left_im, right_re, precision=highest, preferred_element_type=jnp.float32)
    return jnp.stack([real_part, imag_part], 1)


def shards(states_re, states_im):
    kcount = states_re.shape[0]
    bands = states_re.shape[1]
    pw_width = lax.axis_size("pw")
    ka_width = lax.axis_size("ka")
    band_rows = bands // pw_width
    ka_place = lax.axis_index("ka")
    first_band = lax.axis_index("pw") * band_rows
    next_re, next_im = from_behind((states_re[:1], states_im[:1]), "ka", -1)
    after_re = jnp.concatenate([states_re[1:], next_re], 0)
    after_im = jnp.concatenate([states_im[1:], next_im], 0)
    real_part = jnp.einsum(
        "kbg,kcg->bkc", states_re, after_re, preferred_element_type=jnp.float32
    ) + jnp.einsum("kbg,kcg->bkc", states_im, after_im, preferred_element_type=jnp.float32)
    imag_part = jnp.einsum(
        "kbg,kcg->bkc", states_re, after_im, preferred_element_type=jnp.float32
    ) - jnp.einsum("kbg,kcg->bkc", states_im, after_re, preferred_element_type=jnp.float32)
    margin_rows = lax.psum_scatter(
        jnp.stack([real_part, imag_part], 2), "pw", scatter_dimension=0, tiled=True
    )
    margin_full = lax.all_gather(margin_rows, "pw", axis=0, tiled=True)
    row_index = lax.broadcasted_iota(jnp.int32, (band_rows, bands), 0) + first_band
    col_index = lax.broadcasted_iota(jnp.int32, (band_rows, bands), 1)
    eye_real = (row_index == col_index).astype(jnp.float32)
    eye_rows = jnp.stack([eye_real, jnp.zeros_like(eye_real)], 1)

    def sweep(start_rows):
        current = start_rows
        collected = []
        for kpoint in range(kcount):
            current = complex_rows(current, margin_full[:, kpoint])
            collected.append(current)
        return jnp.stack(collected, 0)

    own_span = sweep(eye_rows)[-1]
    span_whole = lax.all_gather(own_span, "pw", axis=0, tiled=True)

    def advance(position, start_rows):
        last_line = complex_rows(start_rows, span_whole)
        received = shifted(last_line, "ka", 1)
        return jnp.where(ka_place == position + 1, received, start_rows)

    start_rows = lax.fori_loop(0, ka_width - 1, advance, eye_rows)
    return sweep(start_rows)


def solution(mesh):
    in_specs = (P("ka", None, "pw"), P("ka", None, "pw"))
    out_specs = P("ka", "pw", None, None)
    return jax.shard_map(shards, mesh=mesh, in_specs=in_specs, out_specs=out_specs, check_vma=False)
```

profile of v0, /device:TPU:8, one launch (start us, length us, event | category | flops | bytes accessed | tf_op | source)
XLA Modules:
  0.0 635.8 jit_solution(6827714051969218923)
XLA Ops:
  6.5 1.9 fusion.87
  8.4 2.7 collective-permute-start.2
  11.3 0.9 collective-permute-start.1
  12.2 22.5 %collective-permute-done.2 = bf16[1,512,1024]{2,1,0:T(8,128)(2,1)S(1)} collective-permute-done((bf16[1,512,1024]{2,1,0:T(8,128)(2,1)S(1)}, bf16[1,512,1024]{2,1,0:T(8,128)(2,1)S(1)}, u32[]{:S(2)}, u32[]{:S(2)}) %collective-permute-start.2) | collective-permute-done | bytes 1048608 | tf_op jit(solution)/shard_map/ppermute | solution.py:10
  34.7 1.3 fusion.20
  36.0 20.1 %collective-permute-done.1 = bf16[1,512,1024]{2,1,0:T(8,128)(2,1)S(1)} collective-permute-done((bf16[1,512,1024]{2,1,0:T(8,128)(2,1)S(1)}, bf16[1,512,1024]{2,1,0:T(8,128)(2,1)S(1)}, u32[]{:S(2)}, u32[]{:S(2)}) %collective-permute-start.1) | collective-permute-done | bytes 1048608 | tf_op jit(solution)/shard_map/ppermute | solution.py:10
  56.0 1.3 fusion.21
  57.3 1.3 add_bitcast_fusion
  58.6 1.3 subtract_bitcast_fusion
  59.9 2.4 pad_maximum_fusion.1
  62.3 7.3 %copy.5 = f32[512,2,2,512]{3,2,1,0:T(2,128)} copy(f32[512,2,2,512]{0,3,1,2:T(8,128)} %pad_maximum_fusion.1) | data formatting | bytes 8388608 | tf_op jit(solution)/shard_map/stack | solution.py:52
  71.6 281.8 %all-reduce.4.cloned.1.call-done = f32[512,2,2,512]{3,2,1,0:T(2,128)} async-done(((f32[512,2,2,512]{3,2,1,0:T(2,128)}), f32[512,2,2,512]{3,2,1,0:T(2,128)}) %all-reduce.4.cloned.1.call-update) | async-done | bytes 4194320
  353.3 1.6 constant_dynamic-slice_fusion
  355.0 86.2 %all-gather.3.cloned.1.call-done = f32[512,2,2,512]{3,2,1,0:T(2,128)} async-done(((f32[16,2,2,512]{3,2,1,0:T(2,128)}), f32[512,2,2,512]{3,2,1,0:T(2,128)}) %all-gather.3.cloned.1.call-update) | async-done | bytes 4194320 | tf_op jit(solution)/shard_map/all_gather | solution.py:54
  441.2 3.7 slice_bitcast_fusion
  444.9 3.5 fusion.85
  450.5 0.6 fusion.36
  453.0 0.6 pad_maximum_fusion.9
  453.8 76.6 %all-gather.5.cloned.1.call-done = f32[512,2,512]{2,0,1:T(8,128)} async-done(((f32[16,2,512]{2,0,1:T(8,128)}), f32[512,2,512]{2,0,1:T(8,128)}) %all-gather.5.cloned.1.call-update) | async-done | bytes 2097168 | tf_op jit(solution)/shard_map/all_gather | solution.py:69
  530.4 3.2 copy.6
  533.6 87.2 %while.13 = (s32[]{:T(128)}, f32[16,2,512]{2,0,1:T(8,128)S(1)}, s32[]{:T(128)}, f32[512,2,512]{2,1,0:T(2,128)S(1)}, s32[]{:T(128)}) while((s32[]{:T(128)}, f32[16,2,512]{2,0,1:T(8,128)S(1)}, s32[]{:T(128)}, f32[512,2,512]{2,1,0:T(2,128)S(1)}, s32[]{:T(128)}) %tuple.40), condition=%wide.region_2.3_spmd, body=%wide.region_1.2_spmd.sunk | while | flops 201375744 | bytes 9306223 | solution.py:76
  533.6 1.6 fusion.122
  537.7 3.4 collective-permute-start
  541.1 4.9 collective-permute-done
  546.0 1.6 fusion.122
  550.1 1.9 collective-permute-start
  552.1 6.3 collective-permute-done
  558.5 1.6 fusion.122
  562.6 1.9 collective-permute-start
  564.5 6.3 collective-permute-done
  570.9 1.6 fusion.122
  575.0 1.9 collective-permute-start
  576.9 6.3 collective-permute-done
  583.3 1.6 fusion.122
  587.4 1.9 collective-permute-start
  589.4 6.3 collective-permute-done
  595.7 1.6 fusion.122
  599.9 1.9 collective-permute-start
  601.8 6.3 collective-permute-done
  608.2 1.6 fusion.122
  612.3 1.9 collective-permute-start
  614.2 6.3 collective-permute-done
  620.8 2.0 fusion.38
  622.8 1.9 fusion.45
  626.6 0.6 convolution_add_fusion.2
  627.2 0.6 fusion.23
  627.9 0.6 fusion.22
  628.5 0.8 copy.7
  (84 shorter events, 25.0 us)
Async XLA Ops:
  6.5 4.6 copy-start.7
  6.5 346.8 %all-reduce.4.cloned.1.call-start = ((), (), s32[]{:S(2)}) async-start(), calls=%async_computation.2 | async-start | bytes 8388608
  8.4 26.3 %copy-start.6 = (bf16[2,512,1024]{2,1,0:T(8,128)(2,1)S(1)}, bf16[2,512,1024]{2,1,0:T(8,128)(2,1)}, u32[]{:S(2)}) copy-start(bf16[2,512,1024]{2,1,0:T(8,128)(2,1)} %param.5) | copy-start | bytes 6291460
  8.4 26.3 %collective-permute-start.2 = (bf16[1,512,1024]{2,1,0:T(8,128)(2,1)S(1)}, bf16[1,512,1024]{2,1,0:T(8,128)(2,1)S(1)}, u32[]{:S(2)}, u32[]{:S(2)}) collective-permute-start(bf16[1,512,1024]{2,1,0:T(8,128)(2,1)S(1)} %get-tuple-element.110), channel_id=1, source_target_pairs={{32,0},{64,32},{96,64},{128,96},{160,128},{192,160},{224,192},{0,2... | collective-permute-start | bytes 3145736 | tf_op jit(solution)/shard_map/ppermute | solution.py:10
  11.3 44.7 %collective-permute-start.1 = (bf16[1,512,1024]{2,1,0:T(8,128)(2,1)S(1)}, bf16[1,512,1024]{2,1,0:T(8,128)(2,1)S(1)}, u32[]{:S(2)}, u32[]{:S(2)}) collective-permute-start(bf16[1,512,1024]{2,1,0:T(8,128)(2,1)S(1)} %get-tuple-element.112), channel_id=1, source_target_pairs={{32,0},{64,32},{96,64},{128,96},{160,128},{192,160},{224,192},{0,2... | collective-permute-start | bytes 3145736 | tf_op jit(solution)/shard_map/ppermute | solution.py:10
  69.7 0.7 copy-start.8
  69.7 371.5 %all-gather.3.cloned.1.call-start = ((), (), s32[]{:S(2)}) async-start(), calls=%async_computation | async-start | bytes 4325376 | tf_op jit(solution)/shard_map/all_gather | solution.py:54
  354.9 175.4 %all-gather.5.cloned.1.call-start = ((), (), s32[]{:S(2)}) async-start(), calls=%async_computation.1 | async-start | bytes 2162688 | tf_op jit(solution)/shard_map/all_gather | solution.py:69
  448.4 2.2 copy-start.2
  448.4 2.2 copy-start.4
  448.4 3.4 copy-start
  537.7 8.3 %collective-permute-start = (f32[16,2,512]{2,0,1:T(8,128)S(1)}, f32[16,2,512]{2,0,1:T(8,128)S(1)}, u32[]{:S(2)}, u32[]{:S(2)}) collective-permute-start(f32[16,2,512]{2,0,1:T(8,128)S(1)} %pad_maximum_fusion.11), channel_id=1, source_target_pairs={{0,32},{32,64},{64,96},{96,128},{128,160},{160,192},{192,224},{1,3... | collective-permute-start | bytes 196616 | tf_op jit(solution)/shard_map/while/body/eval_jaxpr/ppermute | solution.py:16
  550.1 8.3 %collective-permute-start = (f32[16,2,512]{2,0,1:T(8,128)S(1)}, f32[16,2,512]{2,0,1:T(8,128)S(1)}, u32[]{:S(2)}, u32[]{:S(2)}) collective-permute-start(f32[16,2,512]{2,0,1:T(8,128)S(1)} %pad_maximum_fusion.11), channel_id=1, source_target_pairs={{0,32},{32,64},{64,96},{96,128},{128,160},{160,192},{192,224},{1,3... | collective-permute-start | bytes 196616 | tf_op jit(solution)/shard_map/while/body/eval_jaxpr/ppermute | solution.py:16
  562.6 8.3 %collective-permute-start = (f32[16,2,512]{2,0,1:T(8,128)S(1)}, f32[16,2,512]{2,0,1:T(8,128)S(1)}, u32[]{:S(2)}, u32[]{:S(2)}) collective-permute-start(f32[16,2,512]{2,0,1:T(8,128)S(1)} %pad_maximum_fusion.11), channel_id=1, source_target_pairs={{0,32},{32,64},{64,96},{96,128},{128,160},{160,192},{192,224},{1,3... | collective-permute-start | bytes 196616 | tf_op jit(solution)/shard_map/while/body/eval_jaxpr/ppermute | solution.py:16
  575.0 8.3 %collective-permute-start = (f32[16,2,512]{2,0,1:T(8,128)S(1)}, f32[16,2,512]{2,0,1:T(8,128)S(1)}, u32[]{:S(2)}, u32[]{:S(2)}) collective-permute-start(f32[16,2,512]{2,0,1:T(8,128)S(1)} %pad_maximum_fusion.11), channel_id=1, source_target_pairs={{0,32},{32,64},{64,96},{96,128},{128,160},{160,192},{192,224},{1,3... | collective-permute-start | bytes 196616 | tf_op jit(solution)/shard_map/while/body/eval_jaxpr/ppermute | solution.py:16
  587.4 8.3 %collective-permute-start = (f32[16,2,512]{2,0,1:T(8,128)S(1)}, f32[16,2,512]{2,0,1:T(8,128)S(1)}, u32[]{:S(2)}, u32[]{:S(2)}) collective-permute-start(f32[16,2,512]{2,0,1:T(8,128)S(1)} %pad_maximum_fusion.11), channel_id=1, source_target_pairs={{0,32},{32,64},{64,96},{96,128},{128,160},{160,192},{192,224},{1,3... | collective-permute-start | bytes 196616 | tf_op jit(solution)/shard_map/while/body/eval_jaxpr/ppermute | solution.py:16
  599.9 8.3 %collective-permute-start = (f32[16,2,512]{2,0,1:T(8,128)S(1)}, f32[16,2,512]{2,0,1:T(8,128)S(1)}, u32[]{:S(2)}, u32[]{:S(2)}) collective-permute-start(f32[16,2,512]{2,0,1:T(8,128)S(1)} %pad_maximum_fusion.11), channel_id=1, source_target_pairs={{0,32},{32,64},{64,96},{96,128},{128,160},{160,192},{192,224},{1,3... | collective-permute-start | bytes 196616 | tf_op jit(solution)/shard_map/while/body/eval_jaxpr/ppermute | solution.py:16
  612.3 8.3 %collective-permute-start = (f32[16,2,512]{2,0,1:T(8,128)S(1)}, f32[16,2,512]{2,0,1:T(8,128)S(1)}, u32[]{:S(2)}, u32[]{:S(2)}) collective-permute-start(f32[16,2,512]{2,0,1:T(8,128)S(1)} %pad_maximum_fusion.11), channel_id=1, source_target_pairs={{0,32},{32,64},{64,96},{96,128},{128,160},{160,192},{192,224},{1,3... | collective-permute-start | bytes 196616 | tf_op jit(solution)/shard_map/while/body/eval_jaxpr/ppermute | solution.py:16
  620.8 3.9 copy-start.5
  620.8 5.2 copy-start.1
  622.8 3.8 copy-start.3
Sparse Core Ops, SparseCore 0:
  69.8 283.4 all-reduce.3
  356.1 85.0 all-gather.2
  453.8 76.5 all-gather.4
where the time goes:
time: 636 us
  waiting for transfers between devices  530 us (83%)
  matrix products  34.8 us (5%)
  local copies, waits for them, and re-layouts  34.6 us (5%)
  starting transfers between devices  18.6 us (3%)
  between operations  13.9 us (2%)
    unnamed x4, waiting for transfers between devices  282 us
    all_gather x1, waiting for transfers between devices, shards(): margin_full = lax.all_gather(margin_rows, 'pw', axis=0, tiled=True)  86.2 us
    all_gather x1, waiting for transfers between devices, shards(): span_whole = lax.all_gather(own_span, 'pw', axis=0, tiled=True)  76.6 us
    ppermute x7, waiting for transfers between devices, shifted(): return lax.ppermute(shard, axis, pairs)  42.9 us
    ppermute x2, waiting for transfers between devices, from_behind(): return lax.ppermute(block, axis, route)  42.5 us
    ppermute x7, starting transfers between devices, shifted(): return lax.ppermute(shard, axis, pairs)  14.9 us
    slice x8, local copies, waits for them, and re-layouts, complex_rows(): right_re = right[:, 0]  14.8 us
  transfers between devices with their start and end apart: 12, of which 12 were waited for; matrix products, arithmetic and copies ran while one was open for 0% of the time, Pallas kernels for 0%

commit v1 on v0

--- a/solution.py
+++ b/solution.py
@@ -2,6 +2,11 @@
 import jax.numpy as jnp
 from jax import lax
 from jax.sharding import PartitionSpec as P
+from jax.lax import all_to_all, psum
+
+meet_islands = lambda panel: jnp.concatenate(
+    all_to_all(jnp.stack([panel] * psum(1, "pw"), axis=0), "pw", 0, 0), axis=0
+)
 
 
 def from_behind(block, axis, distance):
@@ -51,7 +56,7 @@
     margin_rows = lax.psum_scatter(
         jnp.stack([real_part, imag_part], 2), "pw", scatter_dimension=0, tiled=True
     )
-    margin_full = lax.all_gather(margin_rows, "pw", axis=0, tiled=True)
+    margin_full = meet_islands(margin_rows)
     row_index = lax.broadcasted_iota(jnp.int32, (band_rows, bands), 0) + first_band
     col_index = lax.broadcasted_iota(jnp.int32, (band_rows, bands), 1)
     eye_real = (row_index == col_index).astype(jnp.float32)

time: 636 us -> 659 us (1.036)
  waiting for transfers between devices: 530 us -> 542 us
  starting transfers between devices: 18.6 us -> 25.7 us
    all_to_all x0 -> x1, waiting for transfers between devices: none -> 96.6 us  [all_to_all(jnp.stack([panel] * psum(1, 'pw'), axis=0), 'pw', 0, 0)]
    all_gather x1 -> x0, waiting for transfers between devices: 86.2 us -> none  [shards(): margin_full = lax.all_gather(margin_rows, 'pw', axis=0, tiled=True)]
    all_to_all x0 -> x1, starting transfers between devices: none -> 7.16 us  [all_to_all(jnp.stack([panel] * psum(1, 'pw'), axis=0), 'pw', 0, 0)]
    unnamed x4 -> x3, waiting for transfers between devices: 282 us -> 282 us
where the time goes in v1:
time: 659 us; the launch traced here: 658 us
  waiting for transfers between devices  542 us (82%)
  local copies, waits for them, and re-layouts  37.9 us (6%)
  matrix products  34.8 us (5%)
  starting transfers between devices  25.7 us (4%)
  between operations  14.2 us (2%)
    unnamed x3, waiting for transfers between devices  282 us
    all_to_all x1, waiting for transfers between devices, all_to_all(jnp.stack([panel] * psum(1, 'pw'), axis=0), 'pw', 0, 0)  96.6 us
    all_gather x1, waiting for transfers between devices, shards(): span_whole = lax.all_gather(own_span, 'pw', axis=0, tiled=True)  77.8 us
    ppermute x7, waiting for transfers between devices, shifted(): return lax.ppermute(shard, axis, pairs)  42.9 us
    ppermute x2, waiting for transfers between devices, from_behind(): return lax.ppermute(block, axis, route)  42.5 us
    ppermute x7, starting transfers between devices, shifted(): return lax.ppermute(shard, axis, pairs)  14.9 us
    slice x8, local copies, waits for them, and re-layouts, complex_rows(): right_re = right[:, 0]  14.8 us
  transfers between devices with their start and end apart: 12, of which 12 were waited for; matrix products, arithmetic and copies ran while one was open for 0% of the time, Pallas kernels for 0%

profile of v1, /device:TPU:8, one launch (start us, length us, event | category | flops | bytes accessed | tf_op | source)
XLA Modules:
  0.0 658.2 jit_solution(8680311088206526470)
XLA Ops:
  6.5 1.9 fusion.87
  8.4 2.7 collective-permute-start.2
  11.3 0.9 collective-permute-start.1
  12.2 22.5 %collective-permute-done.2 = bf16[1,512,1024]{2,1,0:T(8,128)(2,1)S(1)} collective-permute-done((bf16[1,512,1024]{2,1,0:T(8,128)(2,1)S(1)}, bf16[1,512,1024]{2,1,0:T(8,128)(2,1)S(1)}, u32[]{:S(2)}, u32[]{:S(2)}) %collective-permute-start.2) | collective-permute-done | bytes 1048608 | tf_op jit(solution)/shard_map/ppermute | solution.py:15
  34.7 1.3 fusion.20
  36.0 20.1 %collective-permute-done.1 = bf16[1,512,1024]{2,1,0:T(8,128)(2,1)S(1)} collective-permute-done((bf16[1,512,1024]{2,1,0:T(8,128)(2,1)S(1)}, bf16[1,512,1024]{2,1,0:T(8,128)(2,1)S(1)}, u32[]{:S(2)}, u32[]{:S(2)}) %collective-permute-start.1) | collective-permute-done | bytes 1048608 | tf_op jit(solution)/shard_map/ppermute | solution.py:15
  56.0 1.3 fusion.21
  57.3 1.3 add_bitcast_fusion
  58.6 1.3 subtract_bitcast_fusion
  59.9 2.4 pad_maximum_fusion.1
  62.3 7.3 %copy.6 = f32[512,2,2,512]{3,2,1,0:T(2,128)} copy(f32[512,2,2,512]{0,3,1,2:T(8,128)} %pad_maximum_fusion.1) | data formatting | bytes 8388608 | tf_op jit(solution)/shard_map/stack | solution.py:57
  69.7 0.6 copy-done.8
  71.6 281.8 %all-reduce.4.cloned.1.call-done = f32[512,2,2,512]{3,2,1,0:T(2,128)} async-done(((f32[512,2,2,512]{3,2,1,0:T(2,128)}), f32[512,2,2,512]{3,2,1,0:T(2,128)}) %all-reduce.4.cloned.1.call-update) | async-done | bytes 4194320
  353.3 0.9 constant_dynamic-slice_fusion
  354.3 3.9 stack.112
  358.2 7.2 %all-to-all-start = ((f32[32,16,2,2,512]{4,3,2,1,0:T(2,128)}), f32[32,16,2,2,512]{4,3,2,1,0:T(2,128)}, u32[]{:S(2)}, u32[]{:S(2)}) async-start(f32[32,16,2,2,512]{4,3,2,1,0:T(2,128)} %stack.112), calls=%async_computation | async-start | bytes 8388608 | tf_op jit(solution)/shard_map/all_to_all | solution.py:8
  365.4 96.6 %all-to-all-done = f32[32,16,2,2,512]{4,3,2,1,0:T(2,128)} async-done(((f32[32,16,2,2,512]{4,3,2,1,0:T(2,128)}), f32[32,16,2,2,512]{4,3,2,1,0:T(2,128)}, u32[]{:S(2)}, u32[]{:S(2)}) %all-to-all-start) | async-done | bytes 4194336 | tf_op jit(solution)/shard_map/all_to_all | solution.py:8
  462.0 3.7 slice_bitcast_fusion
  465.7 3.5 fusion.85
  473.8 0.6 pad_maximum_fusion.9
  474.6 77.8 %all-gather.2.cloned.1.call-done = f32[512,2,512]{2,0,1:T(8,128)} async-done(((f32[16,2,512]{2,0,1:T(8,128)}), f32[512,2,512]{2,0,1:T(8,128)}) %all-gather.2.cloned.1.call-update) | async-done | bytes 2097168 | tf_op jit(solution)/shard_map/all_gather | solution.py:74
  552.4 3.2 copy.7
  555.6 87.2 %while.13 = (s32[]{:T(128)}, f32[16,2,512]{2,0,1:T(8,128)S(1)}, s32[]{:T(128)}, f32[512,2,512]{2,1,0:T(2,128)S(1)}, s32[]{:T(128)}) while((s32[]{:T(128)}, f32[16,2,512]{2,0,1:T(8,128)S(1)}, s32[]{:T(128)}, f32[512,2,512]{2,1,0:T(2,128)S(1)}, s32[]{:T(128)}) %tuple.40), condition=%wide.region_2.3_spmd, body=%wide.region_1.2_spmd.sunk | while | flops 201375744 | bytes 9306223 | solution.py:81
  555.6 1.6 fusion.122
  559.7 3.4 collective-permute-start
  563.1 4.9 collective-permute-done
  568.0 1.6 fusion.122
  572.2 1.9 collective-permute-start
  574.1 6.3 collective-permute-done
  580.5 1.6 fusion.122
  584.6 1.9 collective-permute-start
  586.5 6.3 collective-permute-done
  592.9 1.6 fusion.122
  597.0 1.9 collective-permute-start
  599.0 6.3 collective-permute-done
  605.3 1.6 fusion.122
  609.5 1.9 collective-permute-start
  611.4 6.3 collective-permute-done
  617.8 1.6 fusion.122
  621.9 1.9 collective-permute-start
  623.8 6.3 collective-permute-done
  630.2 1.6 fusion.122
  634.3 1.9 collective-permute-start
  636.3 6.3 collective-permute-done
  642.9 2.0 fusion.38
  644.8 1.9 fusion.45
  648.6 0.6 convolution_add_fusion.2
  650.6 0.8 copy.8
  (84 shorter events, 26.3 us)
Async XLA Ops:
  6.5 4.6 copy-start.7
  6.5 346.8 %all-reduce.4.cloned.1.call-start = ((), (), s32[]{:S(2)}) async-start(), calls=%async_computation.2 | async-start | bytes 8388608
  8.4 26.3 %copy-start.6 = (bf16[2,512,1024]{2,1,0:T(8,128)(2,1)S(1)}, bf16[2,512,1024]{2,1,0:T(8,128)(2,1)}, u32[]{:S(2)}) copy-start(bf16[2,512,1024]{2,1,0:T(8,128)(2,1)} %param.5) | copy-start | bytes 6291460
  8.4 26.3 %collective-permute-start.2 = (bf16[1,512,1024]{2,1,0:T(8,128)(2,1)S(1)}, bf16[1,512,1024]{2,1,0:T(8,128)(2,1)S(1)}, u32[]{:S(2)}, u32[]{:S(2)}) collective-permute-start(bf16[1,512,1024]{2,1,0:T(8,128)(2,1)S(1)} %get-tuple-element.110), channel_id=1, source_target_pairs={{32,0},{64,32},{96,64},{128,96},{160,128},{192,160},{224,192},{0,2... | collective-permute-start | bytes 3145736 | tf_op jit(solution)/shard_map/ppermute | solution.py:15
  11.3 44.7 %collective-permute-start.1 = (bf16[1,512,1024]{2,1,0:T(8,128)(2,1)S(1)}, bf16[1,512,1024]{2,1,0:T(8,128)(2,1)S(1)}, u32[]{:S(2)}, u32[]{:S(2)}) collective-permute-start(bf16[1,512,1024]{2,1,0:T(8,128)(2,1)S(1)} %get-tuple-element.112), channel_id=1, source_target_pairs={{32,0},{64,32},{96,64},{128,96},{160,128},{192,160},{224,192},{0,2... | collective-permute-start | bytes 3145736 | tf_op jit(solution)/shard_map/ppermute | solution.py:15
  69.7 0.7 copy-start.8
  358.2 103.8 %all-to-all-start = ((f32[32,16,2,2,512]{4,3,2,1,0:T(2,128)}), f32[32,16,2,2,512]{4,3,2,1,0:T(2,128)}, u32[]{:S(2)}, u32[]{:S(2)}) async-start(f32[32,16,2,2,512]{4,3,2,1,0:T(2,128)} %stack.112), calls=%async_computation | async-start | bytes 8388608 | tf_op jit(solution)/shard_map/all_to_all | solution.py:8
  365.3 187.1 %all-gather.2.cloned.1.call-start = ((), (), s32[]{:S(2)}) async-start(), calls=%async_computation.1 | async-start | bytes 2162688 | tf_op jit(solution)/shard_map/all_gather | solution.py:74
  469.1 2.2 copy-start.2
  469.1 2.2 copy-start.4
  469.2 3.4 copy-start
  559.7 8.3 %collective-permute-start = (f32[16,2,512]{2,0,1:T(8,128)S(1)}, f32[16,2,512]{2,0,1:T(8,128)S(1)}, u32[]{:S(2)}, u32[]{:S(2)}) collective-permute-start(f32[16,2,512]{2,0,1:T(8,128)S(1)} %pad_maximum_fusion.11), channel_id=1, source_target_pairs={{0,32},{32,64},{64,96},{96,128},{128,160},{160,192},{192,224},{1,3... | collective-permute-start | bytes 196616 | tf_op jit(solution)/shard_map/while/body/eval_jaxpr/ppermute | solution.py:21
  572.2 8.3 %collective-permute-start = (f32[16,2,512]{2,0,1:T(8,128)S(1)}, f32[16,2,512]{2,0,1:T(8,128)S(1)}, u32[]{:S(2)}, u32[]{:S(2)}) collective-permute-start(f32[16,2,512]{2,0,1:T(8,128)S(1)} %pad_maximum_fusion.11), channel_id=1, source_target_pairs={{0,32},{32,64},{64,96},{96,128},{128,160},{160,192},{192,224},{1,3... | collective-permute-start | bytes 196616 | tf_op jit(solution)/shard_map/while/body/eval_jaxpr/ppermute | solution.py:21
  584.6 8.3 %collective-permute-start = (f32[16,2,512]{2,0,1:T(8,128)S(1)}, f32[16,2,512]{2,0,1:T(8,128)S(1)}, u32[]{:S(2)}, u32[]{:S(2)}) collective-permute-start(f32[16,2,512]{2,0,1:T(8,128)S(1)} %pad_maximum_fusion.11), channel_id=1, source_target_pairs={{0,32},{32,64},{64,96},{96,128},{128,160},{160,192},{192,224},{1,3... | collective-permute-start | bytes 196616 | tf_op jit(solution)/shard_map/while/body/eval_jaxpr/ppermute | solution.py:21
  597.0 8.3 %collective-permute-start = (f32[16,2,512]{2,0,1:T(8,128)S(1)}, f32[16,2,512]{2,0,1:T(8,128)S(1)}, u32[]{:S(2)}, u32[]{:S(2)}) collective-permute-start(f32[16,2,512]{2,0,1:T(8,128)S(1)} %pad_maximum_fusion.11), channel_id=1, source_target_pairs={{0,32},{32,64},{64,96},{96,128},{128,160},{160,192},{192,224},{1,3... | collective-permute-start | bytes 196616 | tf_op jit(solution)/shard_map/while/body/eval_jaxpr/ppermute | solution.py:21
  609.5 8.3 %collective-permute-start = (f32[16,2,512]{2,0,1:T(8,128)S(1)}, f32[16,2,512]{2,0,1:T(8,128)S(1)}, u32[]{:S(2)}, u32[]{:S(2)}) collective-permute-start(f32[16,2,512]{2,0,1:T(8,128)S(1)} %pad_maximum_fusion.11), channel_id=1, source_target_pairs={{0,32},{32,64},{64,96},{96,128},{128,160},{160,192},{192,224},{1,3... | collective-permute-start | bytes 196616 | tf_op jit(solution)/shard_map/while/body/eval_jaxpr/ppermute | solution.py:21
  621.9 8.3 %collective-permute-start = (f32[16,2,512]{2,0,1:T(8,128)S(1)}, f32[16,2,512]{2,0,1:T(8,128)S(1)}, u32[]{:S(2)}, u32[]{:S(2)}) collective-permute-start(f32[16,2,512]{2,0,1:T(8,128)S(1)} %pad_maximum_fusion.11), channel_id=1, source_target_pairs={{0,32},{32,64},{64,96},{96,128},{128,160},{160,192},{192,224},{1,3... | collective-permute-start | bytes 196616 | tf_op jit(solution)/shard_map/while/body/eval_jaxpr/ppermute | solution.py:21
  634.3 8.3 %collective-permute-start = (f32[16,2,512]{2,0,1:T(8,128)S(1)}, f32[16,2,512]{2,0,1:T(8,128)S(1)}, u32[]{:S(2)}, u32[]{:S(2)}) collective-permute-start(f32[16,2,512]{2,0,1:T(8,128)S(1)} %pad_maximum_fusion.11), channel_id=1, source_target_pairs={{0,32},{32,64},{64,96},{96,128},{128,160},{160,192},{192,224},{1,3... | collective-permute-start | bytes 196616 | tf_op jit(solution)/shard_map/while/body/eval_jaxpr/ppermute | solution.py:21
  642.8 3.9 copy-start.5
  642.8 5.2 copy-start.1
  644.8 3.8 copy-start.3
Sparse Core Ops, SparseCore 0:
  69.8 283.4 all-reduce.3
  474.6 77.7 all-gather.1
